TPU v7x, 32 devices: a whole 2x2x4 slice. The times are simulated.
32 devices in a mesh: group: 2 (over y), context: 4 (over z), head: 4 (over x, core).
Axes of the slice: x: 2, y: 2, z: 4, core: 2. Of those that a mesh axis runs over, the one named last changes fastest.
Arguments:
- dn_query: bfloat16 [1024, 2048], P(('group', 'context'), 'head'), parts along dimension 0, may hold values from -6 to 6
- dn_key: bfloat16 [1024, 2048], P(('group', 'context'), 'head'), parts along dimension 0, may hold values from -6 to 6
- dn_value: bfloat16 [1024, 4096], P(('group', 'context'), 'head'), parts along dimension 0, may hold values from -6 to 6
- dn_gate: bfloat16 [1024, 4096], P(('group', 'context'), 'head'), parts along dimension 0, may hold values from -6 to 6
- dn_beta_logit: float32 [1024, 32], P(('group', 'context'), 'head'), parts along dimension 0, may hold values from -6 to 6
- dn_decay: float32 [1024, 32], P(('group', 'context'), 'head'), parts along dimension 0, may hold values from -1 to 0
- dn_norm_gain: float32 [128], replicated, may hold values from 0.1 to 1.9
- prefix_state: bfloat16 [4, 32, 128, 128], P('group', 'head', 'context'), parts along dimension 0, may hold values from -6 to 6
- at_query: bfloat16 [1024, 4096], P(('group', 'context'), 'head'), parts along dimension 0, may hold values from -6 to 6
- at_gate: bfloat16 [1024, 4096], P(('group', 'context'), 'head'), parts along dimension 0, may hold values from -6 to 6
- at_key: bfloat16 [1024, 512], P(('group', 'context')), parts along dimension 0, may hold values from -6 to 6
- at_value: bfloat16 [1024, 512], P(('group', 'context')), parts along dimension 0, may hold values from -6 to 6
- prefix_key: bfloat16 [16, 64, 512], P(('group', 'context')), parts along dimension 0, may hold values from -6 to 6
- prefix_value: bfloat16 [16, 64, 512], P(('group', 'context')), parts along dimension 0, may hold values from -6 to 6
- req_len: int32 [8], P('group'), parts along dimension 0, may hold values from 1 to 256, 512 in all
- req_prefix: int32 [8], P('group'), parts along dimension 0, may hold values from 0 to 1, as said below
- req_offset: int32 [8], P('group'), parts along dimension 0, may hold values from 64 to 256, as said below
- block_table: int32 [16], P('group'), parts along dimension 0, may hold values from 0 to 7, each once
Outputs:
- dn_out: bfloat16 [1024, 4096], P(('group', 'context'), 'head'), parts along dimension 0
- at_out: bfloat16 [1024, 4096], P(('group', 'context'), 'head'), parts along dimension 0
There are 2 independent parts, one for each index of `group`. A program takes and returns all parts, laid end to end along the dimension named above; an argument that names none is the same for every part. Nothing has to cross between parts.
Inputs may be any that keep to these rules, and one draw needn't show every extreme that they name: `req_len`: requests lie one after another in row order; the longest has exactly 256 new tokens. `req_prefix`: every prefix is extended by one or more requests. `req_offset`: equal for the requests of one prefix: the number of its cached positions; one prefix holds 256, another from a quarter to a half of 256. `block_table`: entry p * 4 + j is the slot of block j of prefix p; every slot once.
All inputs are finite; a program needn't handle non-finite values.
Results may differ from a plain program's by a relative error of at most 0.011.
Values may be sent and summed in bfloat16 or wider, within the bound.
A program may use at most 128 MiB of HBM per device.

v0:
```python
import math
import jax
import jax.numpy as jnp
from jax import lax
from jax.sharding import PartitionSpec as P

VH = 32
KH = 16
DK = 128
DV = 128
HQ = 16
KVH = 2
HD = 256
ROT = 64
ROPE_THETA = 10000000.0
YARN_FACTOR = 4.0
YARN_ANCHOR = 262144.0
NEG_LARGE = -1e30
HIGH = lax.Precision.HIGHEST


def carried_in(x, axis, join, neutral):
    place = lax.axis_index(axis)
    gathered = jax.tree.map(
        lambda a, kind: lax.all_gather(a.astype(kind), axis),
        x,
        (jnp.bfloat16, jnp.bfloat16, jnp.bfloat16),
    )
    state = jax.tree.map(lambda a, e: jnp.zeros_like(a) + jnp.asarray(e, a.dtype), x, neutral)

    def one(turn, state):
        return join(
            state,
            jax.tree.map(
                lambda a, own: lax.dynamic_index_in_dim(a, turn, 0, False).astype(own.dtype),
                gathered,
                x,
            ),
        )

    return lax.fori_loop(0, place, one, state)


def yarn_tables(positions, rotary):
    half = rotary // 2
    log_theta = math.log(ROPE_THETA)
    lower = max(
        math.floor(rotary * math.log(YARN_ANCHOR / (64.0 * math.pi)) / (2.0 * log_theta)), 0
    )
    upper = min(
        math.ceil(rotary * math.log(YARN_ANCHOR / (2.0 * math.pi)) / (2.0 * log_theta)), rotary - 1
    )
    spread = float(upper - lower)
    index = jnp.arange(half, dtype=jnp.float32)
    plain_frequency = jnp.exp(index * (-2.0 * log_theta / rotary))
    keep = 1.0 - jnp.clip((index - lower) / spread, 0.0, 1.0)
    frequency = plain_frequency * keep + plain_frequency / YARN_FACTOR * (1.0 - keep)
    angles = positions.astype(jnp.float32)[:, None] * frequency[None, :]
    attention_factor = 0.1 * math.log(YARN_FACTOR) + 1.0
    return (jnp.cos(angles) * attention_factor, jnp.sin(angles) * attention_factor)


def rotate(values, cosines, sines, rotary):
    half = rotary // 2
    first = values[..., :half]
    second = values[..., half:rotary]
    cosines = cosines[:, None, :]
    sines = sines[:, None, :]
    return jnp.concatenate(
        [first * cosines - second * sines, second * cosines + first * sines, values[..., rotary:]],
        axis=-1,
    )


def unit_rows(values):
    return values * lax.rsqrt(jnp.sum(values * values, axis=-1, keepdims=True) + 1e-06)


def row_layout(rows, req_len, req_prefix, req_offset):
    starts = jnp.cumsum(req_len) - req_len
    leading_found = (starts[None, :] <= rows[:, None]).astype(jnp.int32)
    segment = jnp.sum(leading_found, axis=1) - 1
    choose = (segment[:, None] == jnp.arange(req_len.shape[0], dtype=jnp.int32)[None, :]).astype(
        jnp.int32
    )
    first = jnp.sum(choose * starts[None, :], axis=1)
    prefix = jnp.sum(choose * req_prefix[None, :], axis=1)
    offset = jnp.sum(choose * req_offset[None, :], axis=1)
    return (segment, first, prefix, offset, offset + rows - first)


def absorb(state, queries, search_handles, values, visible):
    peak, total, summed = state
    scores = jnp.einsum(
        "thd,nd->thn", queries, search_handles, preferred_element_type=jnp.float32
    ) * search_handles.shape[-1] ** (-0.5)
    seen = visible[:, None, :]
    scores = jnp.where(seen, scores, NEG_LARGE)
    new_peak = jnp.maximum(peak, jnp.max(scores, axis=-1))
    weights = jnp.where(seen, jnp.exp(scores - new_peak[..., None]), 0.0)
    shrink = jnp.exp(peak - new_peak)
    total = total * shrink + jnp.sum(weights, axis=-1)
    summed = summed * shrink[..., None] + jnp.einsum(
        "thn,nd->thd", weights.astype(jnp.bfloat16), values, preferred_element_type=jnp.float32
    )
    return (new_peak, total, summed)


def compose(earlier, later):
    map_early, add_early, flag_early = earlier
    map_late, add_late, flag_late = later
    fresh = flag_late > 0.5
    joined_map = jnp.where(
        fresh, map_late, jnp.einsum("hij,hjk->hik", map_early, map_late, precision=HIGH)
    )
    joined_add = jnp.where(
        fresh, add_late, jnp.einsum("hvj,hjk->hvk", add_early, map_late, precision=HIGH) + add_late
    )
    return (joined_map, joined_add, jnp.maximum(flag_early, flag_late))


def shards(
    dn_query,
    dn_key,
    dn_value,
    dn_gate,
    dn_beta_logit,
    dn_decay,
    dn_norm_gain,
    prefix_state,
    at_query,
    at_gate,
    at_key,
    at_value,
    prefix_key,
    prefix_value,
    req_len,
    req_prefix,
    req_offset,
    block_table,
):
    tokens_here = dn_query.shape[0]
    key_heads = dn_query.shape[1] // DK
    value_heads = dn_value.shape[1] // DV
    query_heads = at_query.shape[1] // HD
    device = lax.axis_index("context")
    row_start = device * tokens_here
    rows = row_start + jnp.arange(tokens_here, dtype=jnp.int32)
    segment, first, prefix, offset, position = row_layout(rows, req_len, req_prefix, req_offset)
    query = jnp.repeat(
        unit_rows(dn_query.reshape(tokens_here, key_heads, DK).astype(jnp.float32)) * DK ** (-0.5),
        VH // KH,
        axis=1,
    )
    key = jnp.repeat(
        unit_rows(dn_key.reshape(tokens_here, key_heads, DK).astype(jnp.float32)), VH // KH, axis=1
    )
    query_heads_first = jnp.transpose(query, (1, 0, 2))
    key_heads_first = jnp.transpose(key, (1, 0, 2))
    value_heads_first = jnp.transpose(
        dn_value.reshape(tokens_here, value_heads, DV).astype(jnp.float32), (1, 0, 2)
    )
    beta = jax.nn.sigmoid(dn_beta_logit).T
    same = segment[:, None] == segment[None, :]
    causal = same & (rows[:, None] >= rows[None, :])
    strict = same & (rows[:, None] > rows[None, :])
    running = jnp.dot(causal.astype(jnp.float32), dn_decay, precision=HIGH).T
    gaps = running[:, :, None] - running[:, None, :]
    decay_mat = jnp.where(causal[None], jnp.exp(jnp.where(causal[None], gaps, 0.0)), 0.0)
    key_gram = jnp.einsum("hid,hjd->hij", key_heads_first, key_heads_first, precision=HIGH)
    query_key = jnp.einsum("hid,hjd->hij", query_heads_first, key_heads_first, precision=HIGH)
    lower_mat = jnp.where(strict[None], beta[:, :, None] * key_gram * decay_mat, 0.0)
    system = jnp.eye(tokens_here, dtype=jnp.float32)[None] + lower_mat
    start_decay = jnp.exp(running)
    solve_values = beta[:, :, None] * value_heads_first
    solve_keys = (beta * start_decay)[:, :, None] * key_heads_first
    solved = jax.scipy.linalg.solve_triangular(
        system, jnp.concatenate([solve_values, solve_keys], axis=2), lower=True, unit_diagonal=True
    )
    update = solved[:, :, :DV]
    wy_keys = solved[:, :, DV:]
    mixing = decay_mat * query_key
    local_out = jnp.einsum("hij,hjv->hiv", mixing, update, precision=HIGH)
    reach = start_decay[:, :, None] * query_heads_first - jnp.einsum(
        "hij,hjk->hik", mixing, wy_keys, precision=HIGH
    )
    tail = segment == segment[tokens_here - 1]
    end_gaps = running[:, tokens_here - 1 : tokens_here] - running
    end_weight = jnp.where(tail[None, :], jnp.exp(jnp.where(tail[None, :], end_gaps, 0.0)), 0.0)
    end_decay = start_decay[:, tokens_here - 1]
    identity_mat = jnp.eye(DK, dtype=jnp.float32)
    carry_map = end_decay[:, None, None] * identity_mat[None] - jnp.einsum(
        "hjk,hj,hjl->hkl", wy_keys, end_weight, key_heads_first, precision=HIGH
    )
    carry_add = jnp.einsum("hjv,hj,hjl->hvl", update, end_weight, key_heads_first, precision=HIGH)
    restart = (first[tokens_here - 1] >= row_start).astype(jnp.float32)
    identity = (
        jnp.broadcast_to(identity_mat, (value_heads, DK, DK)),
        jnp.zeros((value_heads, DV, DK), jnp.float32),
        jnp.zeros((), jnp.float32),
    )
    into_map, into_add, into_flag = carried_in(
        (carry_map, carry_add, restart), "context", compose, identity
    )
    carried = ((segment == segment[0]) & (first[0] < row_start))[None, :, None]
    through = jnp.einsum("hkl,hil->hik", into_map, reach, precision=HIGH)
    extra = jnp.einsum("hvk,hik->hiv", into_add, reach, precision=HIGH)
    weight_vec = jnp.where(carried, through, reach).astype(jnp.bfloat16)
    core = local_out + jnp.where(carried, extra, 0.0)
    owner_ids = jnp.arange(prefix_state.shape[0], dtype=jnp.int32)
    select = (prefix[None, :] == owner_ids[:, None]).astype(jnp.bfloat16)
    masked = select[:, None, :, None] * weight_vec[None]
    state_part = jnp.einsum(
        "phik,phvk->hiv",
        masked,
        lax.all_gather(prefix_state, "context", axis=2, tiled=True),
        preferred_element_type=jnp.float32,
    )
    core = core + state_part
    core_rows = jnp.transpose(core, (1, 0, 2))
    normed = core_rows * lax.rsqrt(jnp.mean(core_rows * core_rows, axis=-1, keepdims=True) + 1e-06)
    gate_rows = dn_gate.reshape(tokens_here, value_heads, DV).astype(jnp.float32)
    dn_out = (
        (normed * dn_norm_gain * jax.nn.silu(gate_rows))
        .reshape(tokens_here, value_heads * DV)
        .astype(jnp.bfloat16)
    )
    group = HQ // KVH
    kv_head = lax.axis_index("head") * query_heads // group
    cosines, sines = yarn_tables(position, ROT)
    query_rot = rotate(
        at_query.reshape(tokens_here, query_heads, HD).astype(jnp.float32), cosines, sines, ROT
    ).astype(jnp.bfloat16)
    new_key = lax.dynamic_slice_in_dim(at_key, kv_head * HD, HD, 1).reshape(tokens_here, 1, HD)
    new_key = (
        rotate(new_key.astype(jnp.float32), cosines, sines, ROT)
        .reshape(tokens_here, HD)
        .astype(jnp.bfloat16)
    )
    new_value = lax.dynamic_slice_in_dim(at_value, kv_head * HD, HD, 1)
    cached_key = lax.dynamic_slice_in_dim(prefix_key, kv_head * HD, HD, 2)
    cached_value = lax.dynamic_slice_in_dim(prefix_value, kv_head * HD, HD, 2)
    table_index = jnp.arange(block_table.shape[0], dtype=jnp.int32)
    blocks_per_prefix = block_table.shape[0] // prefix_state.shape[0]
    state = (
        jnp.full((tokens_here, query_heads), NEG_LARGE, jnp.float32),
        jnp.zeros((tokens_here, query_heads), jnp.float32),
        jnp.zeros((tokens_here, query_heads, HD), jnp.float32),
    )
    search_handles = lax.all_gather(cached_key, "context", axis=0, tiled=True)
    values = lax.all_gather(cached_value, "context", axis=0, tiled=True)
    count = search_handles.shape[0]
    width = search_handles.shape[1]
    slots = jnp.arange(count, dtype=jnp.int32)
    entry = jnp.sum(
        jnp.where(block_table[None, :] == slots[:, None], table_index[None, :], 0), axis=1
    )
    owner = jnp.repeat(entry // blocks_per_prefix, width)
    where_in = (
        (entry % blocks_per_prefix)[:, None] * width + jnp.arange(width, dtype=jnp.int32)[None, :]
    ).reshape(count * width)
    visible = (owner[None, :] == prefix[:, None]) & (where_in[None, :] < offset[:, None])
    flat_keys = search_handles.reshape(count * width, search_handles.shape[2])
    flat_values = values.reshape(count * width, values.shape[2])
    state = absorb(state, query_rot, flat_keys, flat_values, visible)
    search_handles = lax.all_gather(new_key, "context", axis=0, tiled=True)
    values = lax.all_gather(new_value, "context", axis=0, tiled=True)
    key_rows = jnp.arange(search_handles.shape[0], dtype=jnp.int32)
    key_segment = row_layout(key_rows, req_len, req_prefix, req_offset)[0]
    visible = (key_segment[None, :] == segment[:, None]) & (key_rows[None, :] <= rows[:, None])
    state = absorb(state, query_rot, search_handles, values, visible)
    peak, total, summed = state
    attention = summed / total[..., None]
    gate_att = at_gate.reshape(tokens_here, query_heads, HD).astype(jnp.float32)
    at_out = (
        (attention * jax.nn.sigmoid(gate_att))
        .reshape(tokens_here, query_heads * HD)
        .astype(jnp.bfloat16)
    )
    return (dn_out, at_out)


def solution(mesh):
    placed = (
        P(("group", "context"), "head"),
        P(("group", "context"), "head"),
        P(("group", "context"), "head"),
        P(("group", "context"), "head"),
        P(("group", "context"), "head"),
        P(("group", "context"), "head"),
        P(),
        P("group", "head", "context", None),
        P(("group", "context"), "head"),
        P(("group", "context"), "head"),
        P(("group", "context"), None),
        P(("group", "context"), None),
        P(("group", "context"), None, None),
        P(("group", "context"), None, None),
        P("group"),
        P("group"),
        P("group"),
        P("group"),
    )
    return jax.shard_map(
        shards,
        mesh=mesh,
        in_specs=placed,
        out_specs=(P(("group", "context"), "head"), P(("group", "context"), "head")),
        check_vma=False,
    )
```

profile of v0, /device:TPU:26, one launch (start us, length us, event | category | flops | bytes accessed | tf_op | source)
XLA Modules:
  0.0 243.3 jit_solution(15976261732324481945)
XLA Ops:
  12.8 2.1 fusion.15
  14.9 79.4 %custom-call.4 = f32[8,1,128,128]{2,3,1,0:T(8,128)S(1)} custom-call(f32[8,1,128,128]{3,2,1,0:T(8,128)} %fusion.15), custom_call_target="InvertDiagBlocksLowerTriangular" | custom-call | tf_op jit(solution)/shard_map/jit(_solve_triangular)/vmap()/triangular_solve | solution.py:177
  94.3 1.8 compare_and_fusion.3
  96.7 1.0 fusion.22
  97.8 1.7 convolution_convert_fusion
  99.8 1.7 fusion.20
  104.2 16.7 %all-gather.2 = bf16[512,1,256]{0,2,1:T(8,128)(2,1)} all-gather(bf16[128,1,256]{0,2,1:T(8,128)(2,1)S(1)} %pad_maximum_fusion.1), channel_id=4, replica_groups=mesh['group'=2,'context'=4,'head'=4] {'context'}, dimensions={0}, use_global_device_ids=true | all-gather | bytes 327680 | tf_op jit(solution)/shard_map/all_gather | solution.py:266
  121.9 16.6 %all_gather.40 = bf16[8,64,256]{2,1,0:T(8,128)(2,1)} all-gather(bf16[2,64,256]{2,1,0:T(8,128)(2,1)S(1)} %constant_dynamic-slice_fusion.3), channel_id=1, replica_groups=mesh['group'=2,'context'=4,'head'=4] {'context'}, dimensions={0}, use_global_device_ids=true | all-gather | bytes 327680 | tf_op jit(solution)/shard_map/all_gather | solution.py:250
  138.9 16.8 %all_gather.41 = bf16[8,64,256]{2,1,0:T(8,128)(2,1)} all-gather(bf16[2,64,256]{2,1,0:T(8,128)(2,1)S(1)} %constant_dynamic-slice_fusion.2), channel_id=1, replica_groups=mesh['group'=2,'context'=4,'head'=4] {'context'}, dimensions={0}, use_global_device_ids=true | all-gather | bytes 327680 | tf_op jit(solution)/shard_map/all_gather | solution.py:251
  155.7 16.5 %all_gather.43 = bf16[512,256]{1,0:T(8,128)(2,1)} all-gather(bf16[128,256]{1,0:T(8,128)(2,1)S(1)} %constant_dynamic-slice_fusion.4), channel_id=1, replica_groups=mesh['group'=2,'context'=4,'head'=4] {'context'}, dimensions={0}, use_global_device_ids=true | all-gather | bytes 327680 | tf_op jit(solution)/shard_map/all_gather | solution.py:267
  172.5 1.0 copy.164
  180.1 1.2 fusion.18
  181.8 1.9 dynamic-update-slice
  183.7 2.3 fusion.19
  186.6 8.6 %all-reduce = bf16[4]{0:T(256)(128)(2,1)} all-reduce(bf16[4]{0:T(256)(128)(2,1)S(1)} %copy-done.39), channel_id=1, replica_groups=mesh['group'=2,'context'=4,'head'=4] {'context'}, use_global_device_ids=true, to_apply=%add | all-reduce | flops 4 | bytes 16
  195.3 1.1 copy.165
  198.4 0.9 copy-done.13
  199.7 15.1 %all_gather.39 = bf16[2,8,128,128]{3,2,0,1:T(8,128)(2,1)S(1)} all-gather(bf16[2,8,32,128]{3,2,0,1:T(8,128)(2,1)S(1)} %copy.150), channel_id=1, replica_groups=mesh['group'=2,'context'=4,'head'=4] {'context'}, dimensions={2}, use_global_device_ids=true | all-gather | bytes 655360 | tf_op jit(solution)/shard_map/all_gather | solution.py:216
  216.1 1.2 convolution_multiply_fusion.3
  217.3 1.5 fusion.43
  220.2 11.2 %while.14 = (s32[]{:T(128)}, f32[8,128,128]{1,2,0:T(8,128)S(1)}, f32[8,128,128]{1,2,0:T(8,128)S(1)}, s32[]{:T(128)}, bf16[4]{0:T(256)(128)(2,1)S(1)}, /*index=5*...) while((s32[]{:T(128)}, f32[8,128,128]{1,2,0:T(8,128)S(1)}, ...), condition=%wide.region_6.7_spmd, body=%wide.region_5.6_spmd.sunk | while | flops 403308544 | bytes 7340196 | solution.py:41
  220.2 1.1 constant_dynamic-slice_fusion.7
  223.9 1.1 constant_dynamic-slice_fusion.7
  227.7 1.1 constant_dynamic-slice_fusion.7
  (191 shorter events, 32.6 us)
Async XLA Ops:
  7.2 96.5 %copy-start = (bf16[128,512]{1,0:T(8,128)(2,1)S(1)}, bf16[128,512]{1,0:T(8,128)(2,1)}, u32[]{:S(2)}) copy-start(bf16[128,512]{1,0:T(8,128)(2,1)} %param.30) | copy-start | bytes 393220
  7.2 212.3 %all-gather.8.cloned.1.call-start = ((), (), s32[]{:S(2)}) async-start(), calls=%async_computation.1 | async-start | bytes 1310720 | tf_op jit(solution)/shard_map/all_gather | solution.py:25
  7.2 3.6 %copy-start.15 = (bf16[128,512]{1,0:T(8,128)(2,1)S(1)}, bf16[128,512]{1,0:T(8,128)(2,1)}, u32[]{:S(2)}) copy-start(bf16[128,512]{1,0:T(8,128)(2,1)} %param.21) | copy-start | bytes 393220
  7.3 92.5 %copy-start.2 = (f32[128,128]{1,0:T(8,128)}, f32[128,128]{1,0:T(8,128)S(1)}, u32[]{:S(2)}) copy-start(f32[128,128]{1,0:T(8,128)S(1)} %get-tuple-element.158) | copy-start | bytes 196612
  9.0 166.3 %copy-start.28 = (s32[128]{0:T(128)}, s32[128]{0:T(128)S(1)}, u32[]{:S(2)}) copy-start(s32[128]{0:T(128)S(1)} %get-tuple-element.108) | copy-start | bytes 1540
  9.0 1.3 copy-start.34
  10.6 85.6 %copy-start.18 = (f32[8,128]{1,0:T(8,128)}, f32[8,128]{1,0:T(8,128)S(1)}, u32[]{:S(2)}) copy-start(f32[8,128]{1,0:T(8,128)S(1)} %convolution_bitcast_fusion.3) | copy-start | bytes 12292
  11.4 1.0 copy-start.10
  96.2 3.4 %copy-start.20 = (f32[8,128]{1,0:T(8,128)}, f32[8,128]{1,0:T(8,128)S(1)}, u32[]{:S(2)}) copy-start(f32[8,128]{1,0:T(8,128)S(1)} %get-tuple-element.135) | copy-start | bytes 12292
  99.5 120.0 %all-gather.6.cloned.1.call-start = ((), (), s32[]{:S(2)}) async-start(), calls=%async_computation | async-start | bytes 1310720 | tf_op jit(solution)/shard_map/all_gather | solution.py:25
  120.9 1.0 copy-start.22
  121.9 16.6 %copy-start.36 = (s32[8]{0:T(128)S(1)}, s32[8]{0:T(128)}, u32[]{:S(2)}) copy-start(s32[8]{0:T(128)} %param.37) | copy-start | bytes 100
  121.9 17.0 %copy-start.23 = (bf16[2,64,512]{2,1,0:T(8,128)(2,1)S(1)}, bf16[2,64,512]{2,1,0:T(8,128)(2,1)}, u32[]{:S(2)}) copy-start(bf16[2,64,512]{2,1,0:T(8,128)(2,1)} %param.33) | copy-start | bytes 393220
  138.9 16.8 %copy-start.24 = (bf16[128,512]{1,0:T(8,128)(2,1)S(1)}, bf16[128,512]{1,0:T(8,128)(2,1)}, u32[]{:S(2)}) copy-start(bf16[128,512]{1,0:T(8,128)(2,1)} %param.31) | copy-start | bytes 393220
  155.7 16.5 %copy-start.12 = (bf16[128,1024]{1,0:T(8,128)(2,1)S(1)}, bf16[128,1024]{1,0:T(8,128)(2,1)}, u32[]{:S(2)}) copy-start(bf16[128,1024]{1,0:T(8,128)(2,1)} %param.29) | copy-start | bytes 786436
  172.5 1.0 copy-start.16
  175.2 1.0 copy-start.14
  178.2 1.9 copy-start.6
  180.1 3.6 %copy-start.4 = (f32[128,4,256]{2,0,1:T(8,128)S(1)}, f32[128,4,256]{2,0,1:T(8,128)}, u32[]{:S(2)}) copy-start(f32[128,4,256]{2,0,1:T(8,128)} %copy.164) | copy-start | bytes 1572868
  183.7 2.3 copy-start.9
  186.0 9.2 %copy-start.3 = (f32[128,128]{1,0:T(8,128)S(1)}, f32[128,128]{1,0:T(8,128)}, u32[]{:S(2)}) copy-start(f32[128,128]{1,0:T(8,128)} %copy-done.2) | copy-start | bytes 196612
  199.7 15.2 %copy-start.29 = (s32[128]{0:T(128)S(1)}, s32[128]{0:T(128)}, u32[]{:S(2)}) copy-start(s32[128]{0:T(128)} %copy-done.28) | copy-start | bytes 1540
  217.3 1.5 copy-start.21
  232.7 1.0 copy-start.1
  (18 other events, 13.3 us)
Sparse Core Ops, SparseCore 0:
  99.7 32.8 all-gather.7
  134.7 33.2 all-gather.5
where the time goes:
time: 244 us; the launch traced here: 243 us
  blocking collectives  90.3 us (37%)
  other arithmetic  87.6 us (36%)
  local copies, waits for them, and re-layouts  27.8 us (11%)
  matrix products  19.2 us (8%)
  between operations  16.1 us (7%)
    another operation x2, other arithmetic, shards(): jax.scipy.linalg.solve_triangular(system, jnp.concatenate([solve_values,...  79.4 us
    all_gather x1, blocking collectives, shards(): values = lax.all_gather(cached_value, 'context', axis=0, tiled=True)  16.8 us
    all_gather x1, blocking collectives, shards(): search_handles = lax.all_gather(new_key, 'context', axis=0, tiled=True)  16.7 us
    all_gather x1, blocking collectives, shards(): search_handles = lax.all_gather(cached_key, 'context', axis=0, tiled=True)  16.6 us
    all_gather x1, blocking collectives, shards(): values = lax.all_gather(new_value, 'context', axis=0, tiled=True)  16.5 us
    unnamed x91, local copies, waits for them, and re-layouts  15.3 us
    all_gather x1, blocking collectives, shards(): lax.all_gather(prefix_state, 'context', axis=2, tiled=True)  15.1 us
    unnamed x1, blocking collectives  8.58 us
  transfers between devices with their start and end apart: 2, of which 0 were waited for; matrix products, arithmetic and copies ran while one was open for 9% of the time, Pallas kernels for 0%

commit v1 on v0

--- a/solution.py
+++ b/solution.py
@@ -139,6 +139,18 @@
     req_offset,
     block_table,
 ):
+
+    def matrix_set(raw, lane_axis, along_dim=0):
+        axis_n = jax.lax.axis_size(lane_axis)
+        inbox = [(m, (m + 1) % axis_n) for m in range(axis_n)]
+        high = [None] * axis_n
+        high[axis_n - 1] = raw
+        for j0 in range(axis_n - 2, -1, -1):
+            high[j0] = jax.lax.ppermute(high[j0 + 1], lane_axis, inbox)
+        tall = jnp.concatenate(high, axis=along_dim)
+        seen_now = (jax.lax.axis_index(lane_axis) + 1) * raw.shape[along_dim]
+        return jnp.roll(tall, seen_now, axis=along_dim)
+
     tokens_here = dn_query.shape[0]
     key_heads = dn_query.shape[1] // DK
     value_heads = dn_value.shape[1] // DV
@@ -264,7 +276,7 @@
     flat_values = values.reshape(count * width, values.shape[2])
     state = absorb(state, query_rot, flat_keys, flat_values, visible)
     search_handles = lax.all_gather(new_key, "context", axis=0, tiled=True)
-    values = lax.all_gather(new_value, "context", axis=0, tiled=True)
+    values = matrix_set(new_value, "context")
     key_rows = jnp.arange(search_handles.shape[0], dtype=jnp.int32)
     key_segment = row_layout(key_rows, req_len, req_prefix, req_offset)[0]
     visible = (key_segment[None, :] == segment[:, None]) & (key_rows[None, :] <= rows[:, None])

time: 244 us -> 227 us (0.930)
  blocking collectives: 90.3 us -> 71.1 us
  starting transfers between devices: 0.08 us -> 6.16 us
  other arithmetic: 87.6 us -> 84.5 us
    all_gather x1 -> x0, blocking collectives: 16.5 us -> none  [shards(): values = lax.all_gather(new_value, 'context', axis=0, tiled=True)]
    ppermute x0 -> x3, starting transfers between devices: none -> 6.08 us  [matrix_set(): high[j0] = jax.lax.ppermute(high[j0 + 1], lane_axis, inbox)]
    unnamed x91 -> x76, local copies, waits for them, and re-layouts: 15.3 us -> 16.9 us
  transfers between devices with their start and end apart: 2 -> 5, of which waited for: 0 -> 0; matrix products, arithmetic and copies ran while one was open for 9% -> 10% of each run, Pallas kernels for 0% -> 0%
where the time goes in v1:
time: 227 us; the launch traced here: 226 us
  other arithmetic  84.5 us (37%)
  blocking collectives  71.1 us (31%)
  local copies, waits for them, and re-layouts  28.5 us (13%)
  matrix products  17.1 us (8%)
  between operations  16 us (7%)
  starting transfers between devices  6.16 us (3%)
    another operation x2, other arithmetic, shards(): jax.scipy.linalg.solve_triangular(system, jnp.concatenate([solve_values,...  78.6 us
    all_gather x1, blocking collectives, shards(): search_handles = lax.all_gather(new_key, 'context', axis=0, tiled=True)  16.9 us
    unnamed x76, local copies, waits for them, and re-layouts  16.9 us
    all_gather x1, blocking collectives, shards(): values = lax.all_gather(cached_value, 'context', axis=0, tiled=True)  16.1 us
    all_gather x1, blocking collectives, shards(): search_handles = lax.all_gather(cached_key, 'context', axis=0, tiled=True)  15.2 us
    all_gather x1, blocking collectives, shards(): lax.all_gather(prefix_state, 'context', axis=2, tiled=True)  14.9 us
    unnamed x1, blocking collectives  8.08 us
    ppermute x3, starting transfers between devices, matrix_set(): high[j0] = jax.lax.ppermute(high[j0 + 1], lane_axis, inbox)  6.08 us
  transfers between devices with their start and end apart: 5, of which 0 were waited for; matrix products, arithmetic and copies ran while one was open for 10% of the time, Pallas kernels for 0%

profile of v1, /device:TPU:26, one launch (start us, length us, event | category | flops | bytes accessed | tf_op | source)
XLA Modules:
  0.0 225.6 jit_solution(9443009363479204883)
XLA Ops:
  12.7 1.3 fusion.15
  14.0 78.6 %custom-call.4 = f32[8,1,128,128]{2,3,1,0:T(8,128)S(1)} custom-call(f32[8,1,128,128]{3,2,1,0:T(8,128)S(1)} %fusion.15), custom_call_target="InvertDiagBlocksLowerTriangular" | custom-call | tf_op jit(solution)/shard_map/jit(_solve_triangular)/vmap()/triangular_solve | solution.py:189
  92.7 1.3 compare_and_fusion.3
  94.6 1.0 fusion.22
  95.6 1.7 convolution_convert_fusion
  98.7 1.7 fusion.20
  103.2 1.2 convolution_multiply_fusion.3
  104.4 1.4 fusion.43
  107.1 16.9 %all-gather.2 = bf16[512,1,256]{0,2,1:T(8,128)(2,1)S(1)} all-gather(bf16[128,1,256]{0,2,1:T(8,128)(2,1)S(1)} %pad_maximum_fusion.1), channel_id=4, replica_groups=mesh['group'=2,'context'=4,'head'=4] {'context'}, dimensions={0}, use_global_device_ids=true | all-gather | bytes 327680 | tf_op jit(solution)/shard_map/all_gather | solution.py:278
  125.0 15.2 %all_gather.37 = bf16[8,64,256]{2,1,0:T(8,128)(2,1)} all-gather(bf16[2,64,256]{2,1,0:T(8,128)(2,1)S(1)} %constant_dynamic-slice_fusion.5), channel_id=1, replica_groups=mesh['group'=2,'context'=4,'head'=4] {'context'}, dimensions={0}, use_global_device_ids=true | all-gather | bytes 327680 | tf_op jit(solution)/shard_map/all_gather | solution.py:262
  140.6 16.1 %all_gather.38 = bf16[8,64,256]{2,1,0:T(8,128)(2,1)S(1)} all-gather(bf16[2,64,256]{2,1,0:T(8,128)(2,1)S(1)} %constant_dynamic-slice_fusion.4), channel_id=1, replica_groups=mesh['group'=2,'context'=4,'head'=4] {'context'}, dimensions={0}, use_global_device_ids=true | all-gather | bytes 327680 | tf_op jit(solution)/shard_map/all_gather | solution.py:263
  159.9 1.2 fusion.18
  161.2 2.2 collective-permute-start.1
  166.7 3.6 %collective-permute-start.2 = (bf16[128,256]{1,0:T(8,128)(2,1)}, bf16[128,256]{1,0:T(8,128)(2,1)}, u32[]{:S(2)}, u32[]{:S(2)}) collective-permute-start(bf16[128,256]{1,0:T(8,128)(2,1)} %collective-permute-done.1), channel_id=1, source_target_pairs={{0,4},{4,8},{8,12},{12,0},{1,5},{5,9},{9,13},{13,1},{2,6},{6,10},{... | collective-permute-start | bytes 196616 | tf_op jit(solution)/shard_map/ppermute | solution.py:149
  170.3 14.9 %all_gather.36 = bf16[2,8,128,128]{3,2,0,1:T(8,128)(2,1)S(1)} all-gather(bf16[2,8,32,128]{3,2,0,1:T(8,128)(2,1)S(1)} %copy.150), channel_id=1, replica_groups=mesh['group'=2,'context'=4,'head'=4] {'context'}, dimensions={2}, use_global_device_ids=true | all-gather | bytes 655360 | tf_op jit(solution)/shard_map/all_gather | solution.py:228
  185.2 8.1 %all-reduce = bf16[4]{0:T(256)(128)(2,1)S(1)} all-reduce(bf16[4]{0:T(256)(128)(2,1)S(1)} %dynamic-update-slice), channel_id=1, replica_groups=mesh['group'=2,'context'=4,'head'=4] {'context'}, use_global_device_ids=true, to_apply=%add | all-reduce | flops 4 | bytes 16
  194.2 1.1 copy.152
  196.4 0.9 constant_dynamic-update-slice_fusion.6
  199.9 1.1 fusion.19
  201.0 1.1 copy.165
  203.0 11.3 %while.14 = (s32[]{:T(128)}, f32[8,128,128]{1,2,0:T(8,128)S(1)}, f32[8,128,128]{1,2,0:T(8,128)S(1)}, s32[]{:T(128)}, bf16[4]{0:T(256)(128)(2,1)S(1)}, /*index=5*...) while((s32[]{:T(128)}, f32[8,128,128]{1,2,0:T(8,128)S(1)}, ...), condition=%wide.region_6.7_spmd, body=%wide.region_5.6_spmd.sunk | while | flops 403308544 | bytes 7340196 | solution.py:41
  203.1 1.1 constant_dynamic-slice_fusion.7
  206.8 1.1 constant_dynamic-slice_fusion.7
  210.6 1.1 constant_dynamic-slice_fusion.7
  (182 shorter events, 33.4 us)
Async XLA Ops:
  7.2 99.4 %copy-start = (bf16[128,512]{1,0:T(8,128)(2,1)S(1)}, bf16[128,512]{1,0:T(8,128)(2,1)}, u32[]{:S(2)}) copy-start(bf16[128,512]{1,0:T(8,128)(2,1)} %param.30) | copy-start | bytes 393220
  7.2 195.8 %all-gather.8.cloned.1.call-start = ((), (), s32[]{:S(2)}) async-start(), calls=%async_computation.1 | async-start | bytes 1310720 | tf_op jit(solution)/shard_map/all_gather | solution.py:25
  7.2 3.5 %copy-start.14 = (bf16[128,512]{1,0:T(8,128)(2,1)S(1)}, bf16[128,512]{1,0:T(8,128)(2,1)}, u32[]{:S(2)}) copy-start(bf16[128,512]{1,0:T(8,128)(2,1)} %param.21) | copy-start | bytes 393220
  9.0 1.2 copy-start.24
  11.3 1.0 copy-start.8
  97.4 105.6 %all-gather.6.cloned.1.call-start = ((), (), s32[]{:S(2)}) async-start(), calls=%async_computation | async-start | bytes 1310720 | tf_op jit(solution)/shard_map/all_gather | solution.py:25
  98.2 63.0 %collective-permute-start = (bf16[128,256]{1,0:T(8,128)(2,1)S(1)}, bf16[128,256]{1,0:T(8,128)(2,1)S(1)}, u32[]{:S(2)}, u32[]{:S(2)}) collective-permute-start(bf16[128,256]{1,0:T(8,128)(2,1)S(1)} %constant_dynamic-slice_fusion.2), channel_id=1, source_target_pairs={{0,4},{4,8},{8,12},{12,0},{1,5},{5,9},{9,13},{13,1},{2,6},{6,10},{... | collective-permute-start | bytes 196616 | tf_op jit(solution)/shard_map/ppermute | solution.py:149
  100.4 0.9 copy-start.9
  101.7 0.9 copy-start.15
  124.0 0.9 copy-start.17
  124.9 34.3 %copy-start.5 = (pred[128,512]{1,0:T(8,128)(4,1)}, pred[128,512]{1,0:T(8,128)(4,1)S(1)}, u32[]{:S(2)}) copy-start(pred[128,512]{1,0:T(8,128)(4,1)S(1)} %fusion.50) | copy-start | bytes 196612
  124.9 15.2 %copy-start.26 = (s32[8]{0:T(128)S(1)}, s32[8]{0:T(128)}, u32[]{:S(2)}) copy-start(s32[8]{0:T(128)} %param.37) | copy-start | bytes 100
  124.9 15.6 %copy-start.18 = (bf16[2,64,512]{2,1,0:T(8,128)(2,1)S(1)}, bf16[2,64,512]{2,1,0:T(8,128)(2,1)}, u32[]{:S(2)}) copy-start(bf16[2,64,512]{2,1,0:T(8,128)(2,1)} %param.33) | copy-start | bytes 393220
  140.1 16.5 %copy-start.10 = (bf16[128,1024]{1,0:T(8,128)(2,1)S(1)}, bf16[128,1024]{1,0:T(8,128)(2,1)}, u32[]{:S(2)}) copy-start(bf16[128,1024]{1,0:T(8,128)(2,1)} %param.29) | copy-start | bytes 786436
  156.8 1.0 copy-start.11
  157.8 0.9 copy-start.4
  161.1 3.5 %copy-start.16 = (bf16[2,8,32,128]{3,2,1,0:T(8,128)(2,1)S(1)}, bf16[2,8,32,128]{3,2,1,0:T(8,128)(2,1)}, u32[]{:S(2)}) copy-start(bf16[2,8,32,128]{3,2,1,0:T(8,128)(2,1)} %param.27) | copy-start | bytes 393220
  161.2 3.4 %copy-start.12 = (bf16[128,256]{1,0:T(8,128)(2,1)}, bf16[128,256]{1,0:T(8,128)(2,1)S(1)}, u32[]{:S(2)}) copy-start(bf16[128,256]{1,0:T(8,128)(2,1)S(1)} %collective-permute-done) | copy-start | bytes 196612
  161.2 5.5 %collective-permute-start.1 = (bf16[128,256]{1,0:T(8,128)(2,1)S(1)}, bf16[128,256]{1,0:T(8,128)(2,1)}, u32[]{:S(2)}, u32[]{:S(2)}) collective-permute-start(bf16[128,256]{1,0:T(8,128)(2,1)S(1)} %collective-permute-done), channel_id=1, source_target_pairs={{0,4},{4,8},{8,12},{12,0},{1,5},{5,9},{9,13},{13,1},{2,6},{6,10},{... | collective-permute-start | bytes 196616 | tf_op jit(solution)/shard_map/ppermute | solution.py:149
  166.7 28.8 %collective-permute-start.2 = (bf16[128,256]{1,0:T(8,128)(2,1)}, bf16[128,256]{1,0:T(8,128)(2,1)}, u32[]{:S(2)}, u32[]{:S(2)}) collective-permute-start(bf16[128,256]{1,0:T(8,128)(2,1)} %collective-permute-done.1), channel_id=1, source_target_pairs={{0,4},{4,8},{8,12},{12,0},{1,5},{5,9},{9,13},{13,1},{2,6},{6,10},{... | collective-permute-start | bytes 196616 | tf_op jit(solution)/shard_map/ppermute | solution.py:149
  195.5 1.8 copy-start.13
  196.4 0.9 copy-start.3
  196.4 2.7 %copy-start.28 = (f32[128,4,256]{2,0,1:T(8,128)S(1)}, f32[128,4,256]{2,0,1:T(8,128)}, u32[]{:S(2)}) copy-start(f32[128,4,256]{2,0,1:T(8,128)} %fusion.18) | copy-start | bytes 1572868
  215.0 1.0 copy-start.1
  (10 other events, 7.3 us)
Sparse Core Ops, SparseCore 0:
  97.5 32.0 all-gather.7
  131.7 32.3 all-gather.5
